TPU v7x, 128 devices: a whole 4x4x4 slice. The times are simulated.
128 devices in a mesh: box: 32 (over y, z, core), tx: 4 (over x).
Axes of the slice: x: 4, y: 4, z: 4, core: 2. Of those that a mesh axis runs over, the one named last changes fastest.
Arguments:
- bank: bfloat16 [512, 1024, 1024], P('box', 'tx'), may hold values from -6 to 6
- pick: int32 [64], replicated, may hold values from 0 to 1023, as said below
- slot_box: int32 [512], replicated, may hold values from 0 to 511, each once
- leaf_factor: bfloat16 [512, 512, 128], P('box'), may hold values from -0.1875 to 0.1875
- self_factor: bfloat16 [9, 512, 64, 128], P(None, 'box'), may hold values from -0.375 to 0.375
- cross_factor: bfloat16 [9, 512, 64, 128], P(None, 'box'), may hold values from -0.375 to 0.375
- target_factor: bfloat16 [512, 64, 4096], P('box'), may hold values from -0.5 to 0.5
Outputs:
- field: bfloat16 [512, 64, 4096], P('box', 'tx')
Inputs may be any that keep to these rules, and one draw needn't show every extreme that they name: `pick`: distinct stored transmitters. `slot_box`: each box once.
All inputs are finite; a program needn't handle non-finite values.
Results may differ from a plain program's by a relative error of at most 0.023.
Values may be sent and summed in bfloat16 or wider, within the bound.
A program may use at most 128 MiB of HBM per device.

v0:
```python
import jax
import jax.numpy as jnp
from jax import lax
from jax.sharding import PartitionSpec as P


def partner_2(block, axis, bit):
    count = lax.axis_size(axis)
    route = []
    for low in range(count):
        high = low | 1 << bit
        if high != low and high < count:
            route += [(low, high), (high, low)]
    return lax.ppermute(block, axis, route)


def complex_times(values, matrix):
    inner = matrix.shape[-2]
    half = matrix.shape[-1] // 2
    first = jnp.einsum(
        "brn,bnk->brk", values[..., :inner], matrix, preferred_element_type=jnp.float32
    )
    second = jnp.einsum(
        "brn,bnk->brk", values[..., inner:], matrix, preferred_element_type=jnp.float32
    )
    return jnp.concatenate(
        [first[..., :half] - second[..., half:], first[..., half:] + second[..., :half]], axis=-1
    )


def per_device(bank, pick, slot_box, leaf_factor, self_factor, cross_factor, target_factor):
    box_dev = bank.shape[0]
    bank_dev = bank.shape[1]
    tx_index = lax.axis_index("tx")
    local_pick = pick - tx_index * bank_dev
    chooser = (local_pick[:, None] == jnp.arange(bank_dev, dtype=jnp.int32)[None, :]).astype(
        jnp.bfloat16
    )
    picked = jnp.einsum("pj,bju->bpu", chooser, bank, preferred_element_type=jnp.float32)
    owned = lax.psum_scatter(picked.astype(jnp.bfloat16), "tx", scatter_dimension=1, tiled=True)
    coefs = complex_times(owned, leaf_factor).astype(jnp.bfloat16)
    box_index = lax.axis_index("box")
    sources = lax.dynamic_slice_in_dim(slot_box, box_index * box_dev, box_dev)
    piece = lax.all_gather(coefs, "box", axis=0, tiled=True)
    count = piece.shape[0]
    taker = (sources[:, None] == jnp.arange(count, dtype=jnp.int32)[None, :]).astype(jnp.bfloat16)
    current = jnp.einsum("sn,nrk->srk", taker, piece, preferred_element_type=jnp.float32).astype(
        jnp.bfloat16
    )
    levels = self_factor.shape[0]
    local_bits = box_dev.bit_length() - 1
    for level in range(levels):
        if level < local_bits:
            span = 1 << level
            shaped = current.reshape(
                box_dev // (2 * span), 2, span, current.shape[1], current.shape[2]
            )
            partner = jnp.flip(shaped, axis=1).reshape(current.shape)
        else:
            partner = partner_2(current, "box", level - local_bits)
        mixed = complex_times(current, self_factor[level]) + complex_times(
            partner, cross_factor[level]
        )
        current = mixed.astype(jnp.bfloat16)
    return complex_times(current, target_factor).astype(jnp.bfloat16)


def solution(mesh):
    in_specs = (
        P("box", "tx", None),
        P(),
        P(),
        P("box", None, None),
        P(None, "box", None, None),
        P(None, "box", None, None),
        P("box", None, None),
    )
    out_specs = P("box", "tx", None)
    return jax.shard_map(
        per_device, mesh=mesh, in_specs=in_specs, out_specs=out_specs, check_vma=False
    )
```

profile of v0, /device:TPU:0, one launch (start us, length us, event | category | flops | bytes accessed | tf_op | source)
XLA Modules:
  0.0 153.6 jit_solution(15288603705547300182)
XLA Ops:
  6.5 0.8 broadcast_subtract_fusion
  7.3 6.3 %convert_bitcast_fusion = bf16[16,64,1024]{2,1,0:T(8,128)(2,1)} fusion(bf16[16,256,1024]{2,1,0:T(8,128)(2,1)} %param.7, s32[64]{0:T(128)S(1)} %broadcast_subtract_fusion), kind=kOutput, calls=%fused_computation.7 | convolution fusion | flops 537935872 | bytes 10486016 | tf_op jit(solution)/shard_map/pj,bju->bpu/dot_general | solution.py:39
  13.8 32.2 %reduce-scatter.2.cloned.1.call-done = bf16[16,16,1024]{2,1,0:T(8,128)(2,1)} async-done(((bf16[16,64,1024]{2,1,0:T(8,128)(2,1)}), bf16[16,16,1024]{2,1,0:T(8,128)(2,1)}) %reduce-scatter.2.cloned.1.call-update) | async-done | bytes 524304 | tf_op jit(solution)/shard_map/reduce_scatter | solution.py:40
  46.0 1.4 fusion.7
  47.4 0.4 fusion.9
  47.9 0.7 pad_maximum_fusion.1
  48.7 0.8 dynamic_slice.3
  49.4 43.1 %all-gather.2.cloned.1.call-done = bf16[512,16,128]{2,1,0:T(8,128)(2,1)} async-done(((bf16[16,16,128]{2,1,0:T(8,128)(2,1)}), bf16[512,16,128]{2,1,0:T(8,128)(2,1)}) %all-gather.2.cloned.1.call-update) | async-done | bytes 2097168 | tf_op jit(solution)/shard_map/all_gather | solution.py:44
  92.6 2.0 %fusion.4 = bf16[16,16,128]{2,0,1:T(8,128)(2,1)S(1)} fusion(bf16[512,16,128]{2,1,0:T(8,128)(2,1)} %all-gather.2.cloned.1.call-done, s32[16]{0:T(128)S(1)} %dynamic_slice.3), kind=kOutput, calls=%fused_computation.8 | convolution fusion | flops 33595392 | bytes 2162752 | tf_op jit(solution)/shard_map/sn,nrk->srk/dot_general | solution.py:47
  94.6 0.3 rev.16
  94.9 1.2 fusion.75
  96.1 1.1 fusion.77
  97.4 1.1 fusion.81
  98.5 1.1 fusion.79
  100.1 1.2 fusion.67
  101.3 1.1 fusion.69
  102.5 1.2 fusion.71
  103.7 1.1 fusion.73
  105.4 1.2 fusion.59
  106.6 1.1 fusion.61
  107.7 1.2 fusion.63
  109.0 1.1 fusion.65
  110.7 1.3 fusion.51
  112.1 1.1 fusion.53
  113.2 1.4 fusion.55
  114.6 1.1 fusion.57
  116.1 0.3 collective-permute-start
  116.5 0.2 fusion.47
  117.0 0.4 collective-permute-done
  117.5 0.2 fusion.43
  118.2 1.3 collective-permute-start.1
  119.5 0.2 fusion.39
  120.0 2.5 %collective-permute-done.1 = bf16[16,16,128]{2,1,0:T(8,128)(2,1)S(1)} collective-permute-done((bf16[16,16,128]{2,1,0:T(8,128)(2,1)S(1)}, bf16[16,16,128]{2,1,0:T(8,128)(2,1)S(1)}, u32[]{:S(2)}, u32[]{:S(2)}) %collective-permute-start.1) | collective-permute-done | bytes 65568 | tf_op jit(solution)/shard_map/ppermute | solution.py:14
  122.5 0.2 fusion.35
  123.3 2.4 %collective-permute-start.2 = (bf16[16,16,128]{2,1,0:T(8,128)(2,1)S(1)}, bf16[16,16,128]{2,1,0:T(8,128)(2,1)S(1)}, u32[]{:S(2)}, u32[]{:S(2)}) collective-permute-start(bf16[16,16,128]{2,1,0:T(8,128)(2,1)S(1)} %fusion.129), channel_id=1, source_target_pairs={{0,16},{16,0},{4,20},{20,4},{8,24},{24,8},{12,28},{28,12},{32,48},... | collective-permute-start | bytes 196616 | tf_op jit(solution)/shard_map/ppermute | solution.py:14
  125.6 0.2 fusion.31
  126.2 2.9 %collective-permute-done.2 = bf16[16,16,128]{2,1,0:T(8,128)(2,1)S(1)} collective-permute-done((bf16[16,16,128]{2,1,0:T(8,128)(2,1)S(1)}, bf16[16,16,128]{2,1,0:T(8,128)(2,1)S(1)}, u32[]{:S(2)}, u32[]{:S(2)}) %collective-permute-start.2) | collective-permute-done | bytes 65568 | tf_op jit(solution)/shard_map/ppermute | solution.py:14
  129.1 0.2 fusion.27
  129.9 1.3 collective-permute-start.3
  131.7 2.5 %collective-permute-done.3 = bf16[16,16,128]{2,1,0:T(8,128)(2,1)S(1)} collective-permute-done((bf16[16,16,128]{2,1,0:T(8,128)(2,1)S(1)}, bf16[16,16,128]{2,1,0:T(8,128)(2,1)S(1)}, u32[]{:S(2)}, u32[]{:S(2)}) %collective-permute-start.3) | collective-permute-done | bytes 65568 | tf_op jit(solution)/shard_map/ppermute | solution.py:14
  134.2 0.2 fusion.19
  134.9 2.7 %collective-permute-start.4 = (bf16[16,16,128]{2,1,0:T(8,128)(2,1)S(1)}, bf16[16,16,128]{2,1,0:T(8,128)(2,1)S(1)}, u32[]{:S(2)}, u32[]{:S(2)}) collective-permute-start(bf16[16,16,128]{2,1,0:T(8,128)(2,1)S(1)} %fusion.131), channel_id=1, source_target_pairs={{0,64},{64,0},{4,68},{68,4},{8,72},{72,8},{12,76},{76,12},{16,80},... | collective-permute-start | bytes 196616 | tf_op jit(solution)/shard_map/ppermute | solution.py:14
  138.2 2.8 %collective-permute-done.4 = bf16[16,16,128]{2,1,0:T(8,128)(2,1)S(1)} collective-permute-done((bf16[16,16,128]{2,1,0:T(8,128)(2,1)S(1)}, bf16[16,16,128]{2,1,0:T(8,128)(2,1)S(1)}, u32[]{:S(2)}, u32[]{:S(2)}) %collective-permute-start.4) | collective-permute-done | bytes 65568 | tf_op jit(solution)/shard_map/ppermute | solution.py:14
  141.0 0.2 fusion.11
  141.7 1.3 fusion.133
  143.0 1.2 fusion.135
  144.2 1.1 fusion.1
  145.3 1.5 pad_maximum_fusion
  (64 shorter events, 6.9 us)
Async XLA Ops:
  6.5 39.4 %copy-start = (bf16[16,512,128]{2,1,0:T(8,128)(2,1)S(1)}, bf16[16,512,128]{2,1,0:T(8,128)(2,1)}, u32[]{:S(2)}) copy-start(bf16[16,512,128]{2,1,0:T(8,128)(2,1)} %param.10) | copy-start | bytes 6291460
  6.5 39.4 %reduce-scatter.2.cloned.1.call-start = ((), (), s32[]{:S(2)}) async-start(), calls=%async_computation.1 | async-start | bytes 2621440 | tf_op jit(solution)/shard_map/reduce_scatter | solution.py:40
  13.7 78.9 %all-gather.2.cloned.1.call-start = ((), (), s32[]{:S(2)}) async-start(), calls=%async_computation.2 | async-start | bytes 2162688 | tf_op jit(solution)/shard_map/all_gather | solution.py:44
  46.0 1.4 copy-start.3
  110.7 5.8 %copy-start.1 = (bf16[9,16,64,128]{3,2,1,0:T(8,128)(2,1)S(1)}, bf16[9,16,64,128]{3,2,1,0:T(8,128)(2,1)}, u32[]{:S(2)}) copy-start(bf16[9,16,64,128]{3,2,1,0:T(8,128)(2,1)} %param.11) | copy-start | bytes 7077892
  113.2 4.3 %copy-start.2 = (bf16[9,16,64,128]{3,2,1,0:T(8,128)(2,1)S(1)}, bf16[9,16,64,128]{3,2,1,0:T(8,128)(2,1)}, u32[]{:S(2)}) copy-start(bf16[9,16,64,128]{3,2,1,0:T(8,128)(2,1)} %param.12) | copy-start | bytes 7077892
  116.1 1.3 collective-permute-start
  118.2 4.3 %collective-permute-start.1 = (bf16[16,16,128]{2,1,0:T(8,128)(2,1)S(1)}, bf16[16,16,128]{2,1,0:T(8,128)(2,1)S(1)}, u32[]{:S(2)}, u32[]{:S(2)}) collective-permute-start(bf16[16,16,128]{2,1,0:T(8,128)(2,1)S(1)} %fusion.128), channel_id=1, source_target_pairs={{0,8},{8,0},{4,12},{12,4},{16,24},{24,16},{20,28},{28,20},{32,40},... | collective-permute-start | bytes 196616 | tf_op jit(solution)/shard_map/ppermute | solution.py:14
  119.9 21.8 %slice-start = ((s8[8388608]{0:T(1024)(128)(4,1)}), s8[4194304]{0:T(1024)(128)(4,1)S(1)}, s32[]{:S(2)}) async-start(s8[8388608]{0:T(1024)(128)(4,1)} %bitcast.120), calls=%async_computation.3 | async-start | bytes 8388608
  123.3 5.8 %collective-permute-start.2 = (bf16[16,16,128]{2,1,0:T(8,128)(2,1)S(1)}, bf16[16,16,128]{2,1,0:T(8,128)(2,1)S(1)}, u32[]{:S(2)}, u32[]{:S(2)}) collective-permute-start(bf16[16,16,128]{2,1,0:T(8,128)(2,1)S(1)} %fusion.129), channel_id=1, source_target_pairs={{0,16},{16,0},{4,20},{20,4},{8,24},{24,8},{12,28},{28,12},{32,48},... | collective-permute-start | bytes 196616 | tf_op jit(solution)/shard_map/ppermute | solution.py:14
  129.8 11.9 %slice-start.1 = ((s8[8388608]{0:T(1024)(128)(4,1)}), s8[4194304]{0:T(1024)(128)(4,1)S(1)}, s32[]{:S(2)}) async-start(s8[8388608]{0:T(1024)(128)(4,1)} %bitcast.120), calls=%async_computation.4 | async-start | bytes 8388608
  129.9 4.3 %collective-permute-start.3 = (bf16[16,16,128]{2,1,0:T(8,128)(2,1)S(1)}, bf16[16,16,128]{2,1,0:T(8,128)(2,1)S(1)}, u32[]{:S(2)}, u32[]{:S(2)}) collective-permute-start(bf16[16,16,128]{2,1,0:T(8,128)(2,1)S(1)} %fusion.130), channel_id=1, source_target_pairs={{0,32},{32,0},{4,36},{36,4},{8,40},{40,8},{12,44},{44,12},{16,48},... | collective-permute-start | bytes 196616 | tf_op jit(solution)/shard_map/ppermute | solution.py:14
  134.9 6.0 %collective-permute-start.4 = (bf16[16,16,128]{2,1,0:T(8,128)(2,1)S(1)}, bf16[16,16,128]{2,1,0:T(8,128)(2,1)S(1)}, u32[]{:S(2)}, u32[]{:S(2)}) collective-permute-start(bf16[16,16,128]{2,1,0:T(8,128)(2,1)S(1)} %fusion.131), channel_id=1, source_target_pairs={{0,64},{64,0},{4,68},{68,4},{8,72},{72,8},{12,76},{76,12},{16,80},... | collective-permute-start | bytes 196616 | tf_op jit(solution)/shard_map/ppermute | solution.py:14
Sparse Core Ops, SparseCore 0:
  13.8 32.0 reduce-scatter.1
  48.8 43.7 all-gather.1
where the time goes:
time: 154 us
  waiting for transfers between devices  86.4 us (56%)
  matrix products  35.8 us (23%)
  between operations  13.9 us (9%)
  other arithmetic  8.3 us (5%)
  starting transfers between devices  7.97 us (5%)
    all_gather x1, waiting for transfers between devices, per_device(): piece = lax.all_gather(coefs, 'box', axis=0, tiled=True)  43.1 us
    reduce_scatter x1, waiting for transfers between devices, per_device(): lax.psum_scatter(picked.astype(jnp.bfloat16), 'tx', scatter_dimension=1,...  32.2 us
    dot_general x20, matrix products, complex_times(): jnp.einsum('brn,bnk->brk', values[..., inner:], matrix, preferred_element...  15 us
    dot_general x20, matrix products, complex_times(): jnp.einsum('brn,bnk->brk', values[..., :inner], matrix, preferred_element...  12.5 us
    ppermute x5, waiting for transfers between devices, partner_2(): return lax.ppermute(block, axis, route)  11 us
    ppermute x5, starting transfers between devices, partner_2(): return lax.ppermute(block, axis, route)  7.93 us
    dot_general x1, matrix products, per_device(): jnp.einsum('pj,bju->bpu', chooser, bank, preferred_element_type=jnp.float32)  6.33 us
  transfers between devices with their start and end apart: 7, of which 7 were waited for; matrix products, arithmetic and copies ran while one was open for 2% of the time, Pallas kernels for 0%

commit v1 on v0

--- a/solution.py
+++ b/solution.py
@@ -41,7 +41,8 @@
     coefs = complex_times(owned, leaf_factor).astype(jnp.bfloat16)
     box_index = lax.axis_index("box")
     sources = lax.dynamic_slice_in_dim(slot_box, box_index * box_dev, box_dev)
-    piece = lax.all_gather(coefs, "box", axis=0, tiled=True)
+    copies = jnp.concatenate([coefs] * lax.axis_size("box"), axis=0)
+    piece = lax.all_to_all(copies, "box", 0, 0, tiled=True)
     count = piece.shape[0]
     taker = (sources[:, None] == jnp.arange(count, dtype=jnp.int32)[None, :]).astype(jnp.bfloat16)
     current = jnp.einsum("sn,nrk->srk", taker, piece, preferred_element_type=jnp.float32).astype(

time: 154 us -> 167 us (1.084)
  local copies, waits for them, and re-layouts: 1.22 us -> 20.9 us
  waiting for transfers between devices: 86.4 us -> 78.2 us
    all_gather x1 -> x0, waiting for transfers between devices: 43.1 us -> none  [per_device(): piece = lax.all_gather(coefs, 'box', axis=0, tiled=True)]
    all_to_all x0 -> x1, waiting for transfers between devices: none -> 28.1 us  [per_device(): piece = lax.all_to_all(copies, 'box', 0, 0, tiled=True)]
    unnamed x12 -> x42, local copies, waits for them, and re-layouts: 0.03 us -> 19 us
    all_to_all x0 -> x1, starting transfers between devices: none -> 7.4 us  [per_device(): piece = lax.all_to_all(copies, 'box', 0, 0, tiled=True)]
    ppermute x5, waiting for transfers between devices: 11 us -> 17.8 us  [partner_2(): return lax.ppermute(block, axis, route)]
    ppermute x5, starting transfers between devices: 7.93 us -> 1.57 us  [partner_2(): return lax.ppermute(block, axis, route)]
where the time goes in v1:
time: 167 us; the launch traced here: 166 us
  waiting for transfers between devices  78.2 us (47%)
  matrix products  35.8 us (21%)
  local copies, waits for them, and re-layouts  20.9 us (13%)
  between operations  13.9 us (8%)
  starting transfers between devices  8.98 us (5%)
  other arithmetic  8.3 us (5%)
    reduce_scatter x1, waiting for transfers between devices, per_device(): lax.psum_scatter(picked.astype(jnp.bfloat16), 'tx', scatter_dimension=1,...  32.2 us
    all_to_all x1, waiting for transfers between devices, per_device(): piece = lax.all_to_all(copies, 'box', 0, 0, tiled=True)  28.1 us
    unnamed x42, local copies, waits for them, and re-layouts  19 us
    ppermute x5, waiting for transfers between devices, partner_2(): return lax.ppermute(block, axis, route)  17.8 us
    dot_general x20, matrix products, complex_times(): jnp.einsum('brn,bnk->brk', values[..., inner:], matrix, preferred_element...  14.8 us
    dot_general x20, matrix products, complex_times(): jnp.einsum('brn,bnk->brk', values[..., :inner], matrix, preferred_element...  12.7 us
    all_to_all x1, starting transfers between devices, per_device(): piece = lax.all_to_all(copies, 'box', 0, 0, tiled=True)  7.4 us
    dot_general x1, matrix products, per_device(): jnp.einsum('pj,bju->bpu', chooser, bank, preferred_element_type=jnp.float32)  6.33 us
  transfers between devices with their start and end apart: 7, of which 7 were waited for; matrix products, arithmetic and copies ran while one was open for 2% of the time, Pallas kernels for 0%

profile of v1, /device:TPU:0, one launch (start us, length us, event | category | flops | bytes accessed | tf_op | source)
XLA Modules:
  0.0 166.1 jit_solution(4934034684158686688)
XLA Ops:
  6.5 0.8 broadcast_subtract_fusion
  7.3 6.3 %convert_bitcast_fusion = bf16[16,64,1024]{2,1,0:T(8,128)(2,1)} fusion(bf16[16,256,1024]{2,1,0:T(8,128)(2,1)} %param.7, s32[64]{0:T(128)S(1)} %broadcast_subtract_fusion), kind=kOutput, calls=%fused_computation.7 | convolution fusion | flops 537935872 | bytes 10486016 | tf_op jit(solution)/shard_map/pj,bju->bpu/dot_general | solution.py:39
  13.7 32.2 %reduce-scatter.2.cloned.1.call-done = bf16[16,16,1024]{2,1,0:T(8,128)(2,1)} async-done(((bf16[16,64,1024]{2,1,0:T(8,128)(2,1)}), bf16[16,16,1024]{2,1,0:T(8,128)(2,1)}) %reduce-scatter.2.cloned.1.call-update) | async-done | bytes 524304 | tf_op jit(solution)/shard_map/reduce_scatter | solution.py:40
  46.0 1.4 fusion.7
  47.9 0.7 constant_dynamic-update-slice_fusion.31
  48.6 0.6 constant_dynamic-update-slice_fusion.30
  49.3 0.6 constant_dynamic-update-slice_fusion.29
  49.9 0.6 constant_dynamic-update-slice_fusion.28
  50.5 0.6 constant_dynamic-update-slice_fusion.27
  51.2 0.6 constant_dynamic-update-slice_fusion.26
  51.8 0.6 constant_dynamic-update-slice_fusion.25
  53.1 0.6 constant_dynamic-update-slice_fusion.23
  54.3 0.6 constant_dynamic-update-slice_fusion.21
  55.6 0.6 constant_dynamic-update-slice_fusion.19
  56.9 0.6 constant_dynamic-update-slice_fusion.17
  65.1 0.6 constant_dynamic-update-slice_fusion.4
  66.4 0.6 constant_dynamic-update-slice_fusion.2
  67.7 0.6 constant_dynamic-update-slice_fusion
  68.3 7.4 %all-to-all-start = ((bf16[512,16,128]{2,1,0:T(8,128)(2,1)}), bf16[512,16,128]{2,1,0:T(8,128)(2,1)}, u32[]{:S(2)}, u32[]{:S(2)}) async-start(bf16[512,16,128]{2,1,0:T(8,128)(2,1)} %constant_dynamic-update-slice_fusion), calls=%async_computation.1 | async-start | bytes 4194304 | tf_op jit(solution)/shard_map/all_to_all | solution.py:45
  75.7 0.8 dynamic_slice.3
  76.5 28.1 %all-to-all-done = bf16[512,16,128]{2,1,0:T(8,128)(2,1)} async-done(((bf16[512,16,128]{2,1,0:T(8,128)(2,1)}), bf16[512,16,128]{2,1,0:T(8,128)(2,1)}, u32[]{:S(2)}, u32[]{:S(2)}) %all-to-all-start) | async-done | bytes 2097184 | tf_op jit(solution)/shard_map/all_to_all | solution.py:45
  104.6 2.0 %fusion.4 = bf16[16,16,128]{2,0,1:T(8,128)(2,1)S(1)} fusion(bf16[512,16,128]{2,1,0:T(8,128)(2,1)} %all-to-all-done, s32[16]{0:T(128)S(1)} %dynamic_slice.3), kind=kOutput, calls=%fused_computation.8 | convolution fusion | flops 33595392 | bytes 2162752 | tf_op jit(solution)/shard_map/sn,nrk->srk/dot_general | solution.py:48
  106.9 1.2 fusion.75
  108.1 1.1 fusion.77
  109.4 1.1 fusion.81
  110.5 1.1 fusion.79
  112.2 1.2 fusion.67
  113.4 1.1 fusion.69
  114.5 1.2 fusion.71
  115.7 1.1 fusion.73
  117.5 1.2 fusion.59
  118.7 1.1 fusion.61
  119.8 1.2 fusion.63
  121.0 1.1 fusion.65
  122.7 1.3 fusion.51
  124.1 1.1 fusion.53
  125.2 1.2 fusion.55
  126.5 1.3 fusion.57
  128.9 0.6 collective-permute-done
  130.9 3.7 %collective-permute-done.1 = bf16[16,16,128]{2,1,0:T(8,128)(2,1)S(1)} collective-permute-done((bf16[16,16,128]{2,1,0:T(8,128)(2,1)S(1)}, bf16[16,16,128]{2,1,0:T(8,128)(2,1)S(1)}, u32[]{:S(2)}, u32[]{:S(2)}) %collective-permute-start.1) | collective-permute-done | bytes 65568 | tf_op jit(solution)/shard_map/ppermute | solution.py:14
  135.3 1.0 collective-permute-start.2
  136.9 4.3 %collective-permute-done.2 = bf16[16,16,128]{2,1,0:T(8,128)(2,1)S(1)} collective-permute-done((bf16[16,16,128]{2,1,0:T(8,128)(2,1)S(1)}, bf16[16,16,128]{2,1,0:T(8,128)(2,1)S(1)}, u32[]{:S(2)}, u32[]{:S(2)}) %collective-permute-start.2) | collective-permute-done | bytes 65568 | tf_op jit(solution)/shard_map/ppermute | solution.py:14
  142.6 4.1 %collective-permute-done.3 = bf16[16,16,128]{2,1,0:T(8,128)(2,1)S(1)} collective-permute-done((bf16[16,16,128]{2,1,0:T(8,128)(2,1)S(1)}, bf16[16,16,128]{2,1,0:T(8,128)(2,1)S(1)}, u32[]{:S(2)}, u32[]{:S(2)}) %collective-permute-start.3) | collective-permute-done | bytes 65568 | tf_op jit(solution)/shard_map/ppermute | solution.py:14
  148.3 5.1 %collective-permute-done.4 = bf16[16,16,128]{2,1,0:T(8,128)(2,1)S(1)} collective-permute-done((bf16[16,16,128]{2,1,0:T(8,128)(2,1)S(1)}, bf16[16,16,128]{2,1,0:T(8,128)(2,1)S(1)}, u32[]{:S(2)}, u32[]{:S(2)}) %collective-permute-start.4) | collective-permute-done | bytes 65568 | tf_op jit(solution)/shard_map/ppermute | solution.py:14
  154.2 1.3 fusion.133
  155.5 1.2 fusion.135
  156.7 1.1 fusion.1
  157.8 1.5 pad_maximum_fusion
  (94 shorter events, 21.4 us)
Async XLA Ops:
  6.5 39.4 %copy-start = (bf16[16,512,128]{2,1,0:T(8,128)(2,1)S(1)}, bf16[16,512,128]{2,1,0:T(8,128)(2,1)}, u32[]{:S(2)}) copy-start(bf16[16,512,128]{2,1,0:T(8,128)(2,1)} %param.10) | copy-start | bytes 6291460
  6.5 39.4 %reduce-scatter.2.cloned.1.call-start = ((), (), s32[]{:S(2)}) async-start(), calls=%async_computation.2 | async-start | bytes 2621440 | tf_op jit(solution)/shard_map/reduce_scatter | solution.py:40
  46.0 1.4 copy-start.3
  68.3 36.3 %all-to-all-start = ((bf16[512,16,128]{2,1,0:T(8,128)(2,1)}), bf16[512,16,128]{2,1,0:T(8,128)(2,1)}, u32[]{:S(2)}, u32[]{:S(2)}) async-start(bf16[512,16,128]{2,1,0:T(8,128)(2,1)} %constant_dynamic-update-slice_fusion), calls=%async_computation.1 | async-start | bytes 4194304 | tf_op jit(solution)/shard_map/all_to_all | solution.py:45
  122.7 5.5 %copy-start.1 = (bf16[9,16,64,128]{3,2,1,0:T(8,128)(2,1)S(1)}, bf16[9,16,64,128]{3,2,1,0:T(8,128)(2,1)}, u32[]{:S(2)}) copy-start(bf16[9,16,64,128]{3,2,1,0:T(8,128)(2,1)} %param.11) | copy-start | bytes 7077892
  126.4 3.1 %copy-start.2 = (bf16[9,16,64,128]{3,2,1,0:T(8,128)(2,1)S(1)}, bf16[9,16,64,128]{3,2,1,0:T(8,128)(2,1)}, u32[]{:S(2)}) copy-start(bf16[9,16,64,128]{3,2,1,0:T(8,128)(2,1)} %param.12) | copy-start | bytes 7077892
  128.2 1.3 collective-permute-start
  130.2 4.3 %collective-permute-start.1 = (bf16[16,16,128]{2,1,0:T(8,128)(2,1)S(1)}, bf16[16,16,128]{2,1,0:T(8,128)(2,1)S(1)}, u32[]{:S(2)}, u32[]{:S(2)}) collective-permute-start(bf16[16,16,128]{2,1,0:T(8,128)(2,1)S(1)} %fusion.128), channel_id=1, source_target_pairs={{0,8},{8,0},{4,12},{12,4},{16,24},{24,16},{20,28},{28,20},{32,40},... | collective-permute-start | bytes 196616 | tf_op jit(solution)/shard_map/ppermute | solution.py:14
  130.8 23.4 %slice-start = ((s8[8388608]{0:T(1024)(128)(4,1)}), s8[4194304]{0:T(1024)(128)(4,1)S(1)}, s32[]{:S(2)}) async-start(s8[8388608]{0:T(1024)(128)(4,1)} %bitcast.120), calls=%async_computation.3 | async-start | bytes 8388608
  135.3 5.8 %collective-permute-start.2 = (bf16[16,16,128]{2,1,0:T(8,128)(2,1)S(1)}, bf16[16,16,128]{2,1,0:T(8,128)(2,1)S(1)}, u32[]{:S(2)}, u32[]{:S(2)}) collective-permute-start(bf16[16,16,128]{2,1,0:T(8,128)(2,1)S(1)} %fusion.129), channel_id=1, source_target_pairs={{0,16},{16,0},{4,20},{20,4},{8,24},{24,8},{12,28},{28,12},{32,48},... | collective-permute-start | bytes 196616 | tf_op jit(solution)/shard_map/ppermute | solution.py:14
  141.9 12.3 %slice-start.1 = ((s8[8388608]{0:T(1024)(128)(4,1)}), s8[4194304]{0:T(1024)(128)(4,1)S(1)}, s32[]{:S(2)}) async-start(s8[8388608]{0:T(1024)(128)(4,1)} %bitcast.120), calls=%async_computation.4 | async-start | bytes 8388608
  141.9 4.8 %collective-permute-start.3 = (bf16[16,16,128]{2,1,0:T(8,128)(2,1)S(1)}, bf16[16,16,128]{2,1,0:T(8,128)(2,1)S(1)}, u32[]{:S(2)}, u32[]{:S(2)}) collective-permute-start(bf16[16,16,128]{2,1,0:T(8,128)(2,1)S(1)} %fusion.130), channel_id=1, source_target_pairs={{0,32},{32,0},{4,36},{36,4},{8,40},{40,8},{12,44},{44,12},{16,48},... | collective-permute-start | bytes 196616 | tf_op jit(solution)/shard_map/ppermute | solution.py:14
  147.4 6.0 %collective-permute-start.4 = (bf16[16,16,128]{2,1,0:T(8,128)(2,1)S(1)}, bf16[16,16,128]{2,1,0:T(8,128)(2,1)S(1)}, u32[]{:S(2)}, u32[]{:S(2)}) collective-permute-start(bf16[16,16,128]{2,1,0:T(8,128)(2,1)S(1)} %fusion.131), channel_id=1, source_target_pairs={{0,64},{64,0},{4,68},{68,4},{8,72},{72,8},{12,76},{76,12},{16,80},... | collective-permute-start | bytes 196616 | tf_op jit(solution)/shard_map/ppermute | solution.py:14
Sparse Core Ops, SparseCore 0:
  13.8 32.0 reduce-scatter.1
